TPU v7x, 32 devices: a whole 2x2x4 slice. The times are simulated.
32 devices in a mesh: groups: 2 (over y), path: 4 (over z), half: 2 (over x), tile: 2 (over core).
Axes of the slice: x: 2, y: 2, z: 4, core: 2. Of those that a mesh axis runs over, the one named last changes fastest.
Arguments:
- left_prefix: bfloat16 [64, 4096], P(('groups', 'path'), ('half', 'tile')), parts along dimension 0, may hold values from -6 to 6
- right_prefix: bfloat16 [64, 4096], P(('groups', 'half', 'tile'), 'path'), parts along dimension 0, may hold values from -6 to 6
- left_layer: bfloat16 [2048, 1024], P(('groups', 'half', 'tile')), parts along dimension 0, may hold values from -0.1875 to 0.1875
- right_layer: bfloat16 [2048, 1024], P(('groups', 'path')), parts along dimension 0, may hold values from -0.1875 to 0.1875
- left_map: int32 [512], P('groups'), parts along dimension 0, may hold values from 0 to 31
- right_map: int32 [512], P('groups'), parts along dimension 0, may hold values from 0 to 31
- branch_bits: int32 [512, 10], P('groups'), parts along dimension 0, may hold values 0 or 1
- cut_side: int32 [20], P('groups'), parts along dimension 0, may hold values 0 or 1
Outputs:
- amplitude: bfloat16 [8192, 4096], P(('groups', 'half', 'tile'), 'path'), parts along dimension 0
There are 2 independent parts, one for each index of `groups`. A program takes and returns all parts, laid end to end along the dimension named above; each array names one. Nothing has to cross between parts.
All inputs are finite; a program needn't handle non-finite values.
Results may differ from a plain program's by a relative error of at most 0.0058.
Values may be sent and summed in bfloat16 or wider, within the bound.
A program may use at most 64 MiB of HBM per device.

v0:
```python
import jax
import jax.numpy as jnp
from jax import lax
from jax.sharding import PartitionSpec as P


def cut_factors(branch, cut_side, gate_count, on_left):
    cut_count = cut_side.shape[0]
    bit_place = lax.broadcasted_iota(jnp.int32, (cut_count, gate_count), 0)
    gate_code = lax.broadcasted_iota(jnp.int32, (cut_count, gate_count), 1)
    bit_table = jnp.right_shift(gate_code, bit_place) & 1
    projector = cut_side if on_left else 1 - cut_side
    phased = 1 - projector
    chosen = branch * projector[None, :]
    misses = (
        jnp.sum(chosen, axis=1, keepdims=True)
        + jnp.dot(projector, bit_table)[None, :]
        - 2 * jnp.dot(chosen, bit_table)
    )
    parity = jnp.dot(branch * phased[None, :], bit_table)
    sign_value = 1 - 2 * (parity % 2)
    return jnp.where(misses == 0, sign_value, 0).astype(jnp.bfloat16)


def project(prefix_rows, path_map, branch, cut_side, on_left):
    factor = cut_factors(branch, cut_side, prefix_rows.shape[1], on_left)
    return prefix_rows[path_map] * factor


def apply_left(projected, left_layer):

    def columns(layer_piece, first_row):
        return lax.dot_general(
            projected, layer_piece, (((1,), (1,)), ((), ())), preferred_element_type=jnp.float32
        )

    states = columns(lax.all_gather(left_layer, ("half", "tile"), axis=0, tiled=True), jnp.int32(0))
    return states.astype(jnp.bfloat16)


def apply_right(projected, right_layer):

    def columns(layer_piece, first_row):
        return lax.dot_general(
            projected, layer_piece, (((1,), (1,)), ((), ())), preferred_element_type=jnp.float32
        )

    states = columns(lax.all_gather(right_layer, "path", axis=0, tiled=True), jnp.int32(0))
    return states.astype(jnp.bfloat16)


def on_device(
    left_prefix, right_prefix, left_layer, right_layer, left_map, right_map, branch_bits, cut_side
):
    left_rows = lax.all_gather(left_prefix, "path", axis=0, tiled=True)
    right_rows = lax.all_gather(right_prefix, ("half", "tile"), axis=0, tiled=True)
    left_states = apply_left(project(left_rows, left_map, branch_bits, cut_side, True), left_layer)
    right_states = apply_right(
        project(right_rows, right_map, branch_bits, cut_side, False), right_layer
    )
    amplitude = lax.dot_general(
        left_states, right_states, (((0,), (0,)), ((), ())), preferred_element_type=jnp.float32
    )
    return amplitude.astype(jnp.bfloat16)


def solution(mesh):
    in_specs = (
        P(("groups", "path"), ("half", "tile")),
        P(("groups", "half", "tile"), "path"),
        P(("groups", "half", "tile"), None),
        P(("groups", "path"), None),
        P("groups"),
        P("groups"),
        P("groups", None),
        P("groups"),
    )
    out_specs = P(("groups", "half", "tile"), "path")
    return jax.shard_map(
        on_device, mesh=mesh, in_specs=in_specs, out_specs=out_specs, check_vma=False
    )
```

profile of v0, /device:TPU:0, one launch (start us, length us, event | category | flops | bytes accessed | tf_op | source)
XLA Modules:
  0.0 92.8 jit_solution(1956754094180607474)
XLA Ops:
  6.5 0.0 all-gather.5.cloned.1.call-start
  6.5 0.7 all-gather.5.cloned.1.call-update
  7.3 0.0 all-gather.3.cloned.1.call-start
  7.3 0.7 all-gather.3.cloned.1.call-update
  8.0 6.5 %all_gather.14 = bf16[32,1024]{1,0:T(8,128)(2,1)S(1)} all-gather(bf16[8,1024]{1,0:T(8,128)(2,1)} %param.9), channel_id=1, replica_groups=mesh['groups'=2,'path'=4,'half'=2,'tile'=2] {'half','tile'}, dimensions={0}, use_global_device_ids=true | all-gather | bytes 81920 | tf_op jit(solution)/shard_map/all_gather | solution.py:56
  14.5 0.7 compare_select_fusion
  15.2 0.0 copy-start.1
  15.2 0.0 copy-start.3
  15.2 1.2 %gather_fusion.1 = bf16[256,1024]{1,0:T(8,128)(2,1)S(1)} fusion(bf16[32,1024]{1,0:T(8,128)(2,1)S(1)} %all_gather.14, s32[1024]{0:T(1024)S(1)} %pad_clamp_fusion), kind=kCustom, calls=%fused_computation.1 | custom fusion | bytes 1049600 | tf_op jit(solution)/shard_map/gather | solution.py:27
  16.3 0.0 copy-done.1
  16.3 14.5 %all_gather.12 = bf16[32,1024]{1,0:T(8,128)(2,1)S(1)} all-gather(bf16[8,1024]{1,0:T(8,128)(2,1)S(1)} %copy-done.1), channel_id=1, replica_groups=mesh['groups'=2,'path'=4,'half'=2,'tile'=2] {'path'}, dimensions={0}, use_global_device_ids=true | all-gather | bytes 81920 | tf_op jit(solution)/shard_map/all_gather | solution.py:55
  30.8 0.0 copy-done.3
  30.8 0.0 copy-start.2
  30.9 0.0 copy-start
  30.9 1.2 %gather_fusion = bf16[256,1024]{1,0:T(8,128)(2,1)S(1)} fusion(bf16[32,1024]{1,0:T(8,128)(2,1)S(1)} %all_gather.12, s32[1024]{0:T(1024)S(1)} %pad_clamp_fusion.1), kind=kCustom, calls=%fused_computation | custom fusion | bytes 1049600 | tf_op jit(solution)/shard_map/gather | solution.py:27
  32.0 0.0 copy-done.2
  32.1 0.0 copy-done
  32.1 0.1 multiply_reduce_fusion.1
  32.2 0.2 fusion.28
  32.3 0.2 fusion.31
  32.5 1.7 %fusion.29 = s32[256,1024]{1,0:T(8,128)S(1)} fusion(s32[256,10]{0,1:T(8,128)S(1)} %copy-done, s32[10]{0:T(128)S(1)} %broadcast_subtract_fusion), kind=kOutput, calls=%fused_computation.35 | convolution fusion | flops 5265920 | bytes 1058856 | tf_op jit(solution)/shard_map/dot_general | solution.py:20
  34.2 1.7 %fusion.30 = s32[256,1024]{1,0:T(8,128)S(1)} fusion(s32[256,10]{0,1:T(8,128)S(1)} %copy-done, s32[10]{0:T(128)S(1)} %copy-done.2), kind=kOutput, calls=%fused_computation.36 | convolution fusion | flops 5265920 | bytes 1058856 | tf_op jit(solution)/shard_map/dot_general | solution.py:18
  35.9 22.1 %all-gather.5.cloned.1.call-done = bf16[1024,1024]{1,0:T(8,128)(2,1)} async-done(((bf16[256,1024]{1,0:T(8,128)(2,1)}), bf16[1024,1024]{1,0:T(8,128)(2,1)}) %all-gather.5.cloned.1.call-update) | async-done | bytes 2097168 | tf_op jit(solution)/shard_map/all_gather | solution.py:48
  58.0 3.6 %convolution_convert_fusion.1 = bf16[256,1024]{1,0:T(8,128)(2,1)} fusion(bf16[1024,1024]{1,0:T(8,128)(2,1)} %all-gather.5.cloned.1.call-done, bf16[256,1024]{1,0:T(8,128)(2,1)S(1)} %gather_fusion.1, s32[256,1024]{1,0:T(8,128)S(1)} %fusion.29, s32[256,1024]{1,0:T(8,128)S(1)} %fusion.30, s32[1024]{0:T(1024)S(1)} %bitcast.12, s32[256]{0:T(256)S(1)} %get-tuple-element.6), kind=kOutput, calls=%fused_computation.9 | convolution fusion | flops 543162368 | bytes 5248000 | tf_op jit(solution)/shard_map/dot_general | solution.py:44
  61.7 19.5 %all-gather.3.cloned.1.call-done = bf16[1024,1024]{1,0:T(8,128)(2,1)} async-done(((bf16[256,1024]{1,0:T(8,128)(2,1)}), bf16[1024,1024]{1,0:T(8,128)(2,1)}) %all-gather.3.cloned.1.call-update) | async-done | bytes 2097168 | tf_op jit(solution)/shard_map/all_gather | solution.py:37
  81.2 4.8 %convolution_convert_fusion = bf16[1024,1024]{1,0:T(8,128)(2,1)} fusion(bf16[256,1024]{1,0:T(8,128)(2,1)} %convolution_convert_fusion.1, bf16[1024,1024]{1,0:T(8,128)(2,1)} %all-gather.3.cloned.1.call-done, bf16[256,1024]{1,0:T(8,128)(2,1)S(1)} %gather_fusion, s32[256,1024]{1,0:T(8,128)S(1)} %fusion.30, s32[256,1024]{1,0:T(8,128)S(1)} %fusion.29, ...), kind=kOutput, calls=%fused_computation.2 | convolution fusion | flops 1081081856 | bytes 7345152 | tf_op jit(solution)/shard_map/dot_general | solution.py:61
  (4 shorter events, 0.0 us)
Async XLA Ops:
  6.5 51.5 %all-gather.5.cloned.1.call-start = ((), (), s32[]{:S(2)}) async-start(), calls=%async_computation.1 | async-start | bytes 2621440 | tf_op jit(solution)/shard_map/all_gather | solution.py:48
  7.3 73.9 %all-gather.3.cloned.1.call-start = ((), (), s32[]{:S(2)}) async-start(), calls=%async_computation | async-start | bytes 2621440 | tf_op jit(solution)/shard_map/all_gather | solution.py:37
  15.2 1.2 %copy-start.1 = (bf16[8,1024]{1,0:T(8,128)(2,1)S(1)}, bf16[8,1024]{1,0:T(8,128)(2,1)}, u32[]{:S(2)}) copy-start(bf16[8,1024]{1,0:T(8,128)(2,1)} %param.8) | copy-start | bytes 49156
  15.2 15.7 %copy-start.3 = (s32[256]{0:T(256)S(1)}, s32[256]{0:T(256)}, u32[]{:S(2)}) copy-start(s32[256]{0:T(256)} %param.12) | copy-start | bytes 3076
  30.8 1.2 %copy-start.2 = (s32[10]{0:T(128)S(1)}, s32[10]{0:T(128)}, u32[]{:S(2)}) copy-start(s32[10]{0:T(128)} %param.15) | copy-start | bytes 124
  30.9 1.2 %copy-start = (s32[256,10]{0,1:T(8,128)S(1)}, s32[256,10]{0,1:T(8,128)}, u32[]{:S(2)}) copy-start(s32[256,10]{0,1:T(8,128)} %param.14) | copy-start | bytes 30724
Sparse Core Ops, SparseCore 0:
  8.9 49.0 all-gather.4
  59.6 21.5 all-gather.2
where the time goes:
time: 93 us; the launch traced here: 92.8 us
  waiting for transfers between devices  43 us (46%)
  blocking collectives  20.9 us (22%)
  between operations  13.5 us (15%)
  matrix products  12.2 us (13%)
  local copies, waits for them, and re-layouts  2.36 us (3%)
    all_gather x1, waiting for transfers between devices, apply_right(): lax.all_gather(right_layer, 'path', axis=0, tiled=True)  22.1 us
    all_gather x1, waiting for transfers between devices, apply_left(): lax.all_gather(left_layer, ('half', 'tile'), axis=0, tiled=True)  19.5 us
    all_gather x1, blocking collectives, on_device(): left_rows = lax.all_gather(left_prefix, 'path', axis=0, tiled=True)  14.5 us
    all_gather x1, blocking collectives, on_device(): lax.all_gather(right_prefix, ('half', 'tile'), axis=0, tiled=True)  6.46 us
    dot_general x1, matrix products, on_device(): lax.dot_general(left_states, right_states, (((0,), (0,)), ((), ())), pref...  4.84 us
    dot_general x1, matrix products, columns(): lax.dot_general(projected, layer_piece, (((1,), (1,)), ((), ())), preferr...  3.64 us
    gather x2, local copies, waits for them, and re-layouts, project(): return prefix_rows[path_map] * factor  2.34 us
  transfers between devices with their start and end apart: 2, of which 2 were waited for; matrix products, arithmetic and copies ran while one was open for 11% of the time, Pallas kernels for 0%

commit v1 on v0

--- a/solution.py
+++ b/solution.py
@@ -2,6 +2,22 @@
 import jax.numpy as jnp
 from jax import lax
 from jax.sharding import PartitionSpec as P
+
+
+def gather_around(x, axis, dim):
+    ways, here, step = (lax.axis_size(axis), lax.axis_index(axis), x.shape[dim])
+    shape = [n * ways if d == dim else n for d, n in enumerate(x.shape)]
+    full = lax.dynamic_update_slice_in_dim(jnp.zeros(shape, x.dtype), x, here * step, axis=dim)
+    going_up = going_down = x
+    for far in range(1, ways // 2 + 1):
+        going_up = lax.ppermute(going_up, axis, [(d, (d + 1) % ways) for d in range(ways)])
+        full = lax.dynamic_update_slice_in_dim(full, going_up, (here - far) % ways * step, axis=dim)
+        if 2 * far < ways:
+            going_down = lax.ppermute(going_down, axis, [(d, (d - 1) % ways) for d in range(ways)])
+            full = lax.dynamic_update_slice_in_dim(
+                full, going_down, (here + far) % ways * step, axis=dim
+            )
+    return full
 
 
 def cut_factors(branch, cut_side, gate_count, on_left):
@@ -45,7 +61,7 @@
             projected, layer_piece, (((1,), (1,)), ((), ())), preferred_element_type=jnp.float32
         )
 
-    states = columns(lax.all_gather(right_layer, "path", axis=0, tiled=True), jnp.int32(0))
+    states = columns(gather_around(right_layer, "path", 0), jnp.int32(0))
     return states.astype(jnp.bfloat16)
 
 

time: 93 us -> 76.5 us (0.82)
  waiting for transfers between devices: 43 us -> 0.72 us
  blocking collectives: 20.9 us -> 34.2 us
  local copies, waits for them, and re-layouts: 2.36 us -> 7.86 us
  starting transfers between devices: 0.04 us -> 5.26 us
  other arithmetic: 0.79 us -> 2.12 us
    all_gather x1 -> x0, waiting for transfers between devices: 22.1 us -> none  [apply_right(): lax.all_gather(right_layer, 'path', axis=0, tiled=True)]
    all_gather x1, waiting for transfers between devices: 19.5 us -> 0.01 us  [apply_left(): lax.all_gather(left_layer, ('half', 'tile'), axis=0, tiled=True)]
    all_gather x1, blocking collectives: 14.5 us -> 28.8 us  [on_device(): left_rows = lax.all_gather(left_prefix, 'path', axis=0, tiled=True)]
    ppermute x0 -> x3, starting transfers between devices: none -> 5.26 us  [the longest x2 3.16 us: gather_around(): lax.ppermute(going_up, axis, [(d, (d + 1) % ways) for d in range(ways)])]
    dynamic_update_slice x0 -> x4, local copies, waits for them, and re-layouts: none -> 3.67 us  [the longest x2 2.54 us: gather_around(): lax.dynamic_update_slice_in_dim(full, going_up, (here - far) % ways * ste...]
    gather x2, local copies, waits for them, and re-layouts: 2.34 us -> 3.91 us  [project(): return prefix_rows[path_map] * factor]
    dot_general x1, matrix products: 3.64 us -> 2.07 us  [columns(): lax.dot_general(projected, layer_piece, (((1,), (1,)), ((), ())), preferr...]
    dot_general x2, matrix products: 0.37 us -> 1.69 us  [cut_factors(): jnp.dot(projector, bit_table)[None, :]]
  transfers between devices with their start and end apart: 2 -> 4, of which waited for: 2 -> 0; matrix products, arithmetic and copies ran while one was open for 11% -> 22% of each run, Pallas kernels for 0% -> 0%
where the time goes in v1:
time: 76.5 us; the launch traced here: 76.2 us
  blocking collectives  34.2 us (45%)
  between operations  13.6 us (18%)
  matrix products  12.4 us (16%)
  local copies, waits for them, and re-layouts  7.86 us (10%)
  starting transfers between devices  5.26 us (7%)
  other arithmetic  2.12 us (3%)
    all_gather x1, blocking collectives, on_device(): left_rows = lax.all_gather(left_prefix, 'path', axis=0, tiled=True)  28.8 us
    all_gather x1, blocking collectives, on_device(): lax.all_gather(right_prefix, ('half', 'tile'), axis=0, tiled=True)  5.45 us
    dot_general x1, matrix products, on_device(): lax.dot_general(left_states, right_states, (((0,), (0,)), ((), ())), pref...  5.32 us
    gather x2, local copies, waits for them, and re-layouts, project(): return prefix_rows[path_map] * factor  3.91 us
    ppermute x2, starting transfers between devices, gather_around(): lax.ppermute(going_up, axis, [(d, (d + 1) % ways) for d in range(ways)])  3.16 us
    dynamic_update_slice x2, local copies, waits for them, and re-layouts, gather_around(): lax.dynamic_update_slice_in_dim(full, going_up, (here - far) % ways * ste...  2.54 us
    ppermute x1, starting transfers between devices, gather_around(): lax.ppermute(going_down, axis, [(d, (d - 1) % ways) for d in range(ways)])  2.09 us
    dot_general x1, matrix products, columns(): lax.dot_general(projected, layer_piece, (((1,), (1,)), ((), ())), preferr...  2.07 us
  transfers between devices with their start and end apart: 4, of which 0 were waited for; matrix products, arithmetic and copies ran while one was open for 22% of the time, Pallas kernels for 0%

profile of v1, /device:TPU:0, one launch (start us, length us, event | category | flops | bytes accessed | tf_op | source)
XLA Modules:
  0.0 76.2 jit_solution(9448678437118422326)
XLA Ops:
  6.5 0.0 all-gather.2.cloned.1.call-start
  6.5 0.7 all-gather.2.cloned.1.call-update
  7.3 3.1 %collective-permute-start = (bf16[256,1024]{1,0:T(8,128)(2,1)}, bf16[256,1024]{1,0:T(8,128)(2,1)}, u32[]{:S(2)}, u32[]{:S(2)}) collective-permute-start(bf16[256,1024]{1,0:T(8,128)(2,1)} %param.11), channel_id=1, source_target_pairs={{0,4},{4,8},{8,12},{12,0},{1,5},{5,9},{9,13},{13,1},{2,6},{6,10},{... | collective-permute-start | bytes 1572872 | tf_op jit(solution)/shard_map/ppermute | solution.py:13
  10.4 2.1 %collective-permute-start.1 = (bf16[256,1024]{1,0:T(8,128)(2,1)}, bf16[256,1024]{1,0:T(8,128)(2,1)}, u32[]{:S(2)}, u32[]{:S(2)}) collective-permute-start(bf16[256,1024]{1,0:T(8,128)(2,1)} %param.11), channel_id=1, source_target_pairs={{0,12},{4,0},{8,4},{12,8},{1,13},{5,1},{9,5},{13,9},{2,14},{6,2},{... | collective-permute-start | bytes 1572872 | tf_op jit(solution)/shard_map/ppermute | solution.py:16
  12.5 0.7 compare_select_fusion
  13.1 0.7 broadcast_subtract_fusion
  13.8 0.7 compare_select_fusion.1
  14.5 0.8 %fusion.28 = s32[1,1024]{1,0:T(1,128)S(1)} fusion(s32[10]{0:T(128)} %param.15), kind=kOutput, calls=%fused_computation.34 | convolution fusion | flops 40970 | bytes 4136 | tf_op jit(solution)/shard_map/dot_general | solution.py:33
  15.3 0.8 %fusion.31 = s32[1,1024]{1,0:T(1,128)S(1)} fusion(s32[10]{0:T(128)} %param.15), kind=kOutput, calls=%fused_computation.37 | convolution fusion | flops 40960 | bytes 4136 | tf_op jit(solution)/shard_map/dot_general | solution.py:33
  16.3 5.4 %all_gather.11 = bf16[32,1024]{1,0:T(8,128)(2,1)S(1)} all-gather(bf16[8,1024]{1,0:T(8,128)(2,1)} %param.9), channel_id=1, replica_groups=mesh['groups'=2,'path'=4,'half'=2,'tile'=2] {'half','tile'}, dimensions={0}, use_global_device_ids=true | all-gather | bytes 81920 | tf_op jit(solution)/shard_map/all_gather | solution.py:72
  21.7 2.0 %gather_fusion.1 = bf16[256,1024]{1,0:T(8,128)(2,1)} fusion(bf16[32,1024]{1,0:T(8,128)(2,1)S(1)} %all_gather.11, s32[1024]{0:T(1024)S(1)} %pad_clamp_fusion), kind=kCustom, calls=%fused_computation.1 | custom fusion | bytes 1049600 | tf_op jit(solution)/shard_map/gather | solution.py:43
  23.7 0.0 copy-done.3
  23.7 0.0 copy-done.5
  23.7 0.1 multiply_reduce_fusion.1
  23.8 1.7 %fusion.29 = s32[256,1024]{1,0:T(8,128)S(1)} fusion(s32[256,10]{0,1:T(8,128)S(1)} %copy-done.3, s32[10]{0:T(128)S(1)} %broadcast_subtract_fusion), kind=kOutput, calls=%fused_computation.35 | convolution fusion | flops 5265920 | bytes 1058856 | tf_op jit(solution)/shard_map/dot_general | solution.py:36
  25.4 0.3 broadcast_in_dim.11
  25.7 0.0 copy-done.2
  25.8 0.0 collective-permute-done
  25.8 0.1 collective-permute-start.2
  25.9 0.0 copy-done.4
  25.9 28.8 %all_gather.9 = bf16[32,1024]{1,0:T(8,128)(2,1)S(1)} all-gather(bf16[8,1024]{1,0:T(8,128)(2,1)S(1)} %copy-done.4), channel_id=1, replica_groups=mesh['groups'=2,'path'=4,'half'=2,'tile'=2] {'path'}, dimensions={0}, use_global_device_ids=true | all-gather | bytes 81920 | tf_op jit(solution)/shard_map/all_gather | solution.py:71
  54.6 2.0 %gather_fusion = bf16[256,1024]{1,0:T(8,128)(2,1)} fusion(bf16[32,1024]{1,0:T(8,128)(2,1)S(1)} %all_gather.9, s32[1024]{0:T(1024)S(1)} %pad_clamp_fusion.1), kind=kCustom, calls=%fused_computation | custom fusion | bytes 1049600 | tf_op jit(solution)/shard_map/gather | solution.py:43
  56.6 1.7 %fusion.30 = s32[256,1024]{1,0:T(8,128)S(1)} fusion(s32[256,10]{0,1:T(8,128)S(1)} %copy-done.3, s32[10]{0:T(128)S(1)} %copy-done.5), kind=kOutput, calls=%fused_computation.36 | convolution fusion | flops 5265920 | bytes 1058856 | tf_op jit(solution)/shard_map/dot_general | solution.py:34
  58.3 0.0 copy-start
  58.3 1.5 %constant_dynamic-update-slice_fusion.2 = bf16[1024,1024]{1,0:T(8,128)(2,1)S(1)} fusion(bf16[1024,1024]{1,0:T(8,128)(2,1)S(1)} %constant_dynamic-update-slice_fusion.3, bf16[256,1024]{1,0:T(8,128)(2,1)} %collective-permute-done, s32[]{:T(128)S(6)} %select_n.58), kind=kLoop, calls=%fused_computation.55 | loop fusion | bytes 1048580 | tf_op jit(solution)/shard_map/dynamic_update_slice | solution.py:14
  59.7 0.0 collective-permute-done.1
  59.8 1.1 %constant_dynamic-update-slice_fusion.1 = bf16[1024,1024]{1,0:T(8,128)(2,1)S(1)} fusion(bf16[1024,1024]{1,0:T(8,128)(2,1)S(1)} %constant_dynamic-update-slice_fusion.2, bf16[256,1024]{1,0:T(8,128)(2,1)} %collective-permute-done.1, s32[]{:T(128)S(6)} %select_n.60), kind=kLoop, calls=%fused_computation.54 | loop fusion | bytes 1048580 | tf_op jit(solution)/shard_map/dynamic_update_slice | solution.py:17
  60.8 0.0 collective-permute-done.2
  60.9 1.1 %constant_dynamic-update-slice_fusion = bf16[1024,1024]{1,0:T(8,128)(2,1)S(1)} fusion(bf16[1024,1024]{1,0:T(8,128)(2,1)S(1)} %constant_dynamic-update-slice_fusion.1, bf16[256,1024]{1,0:T(8,128)(2,1)} %collective-permute-done.2, s32[]{:T(128)S(6)} %select_n.62), kind=kLoop, calls=%fused_computation.53 | loop fusion | bytes 1048580 | tf_op jit(solution)/shard_map/dynamic_update_slice | solution.py:14
  61.9 0.0 copy-done
  62.0 2.1 %convolution_convert_fusion.1 = bf16[256,1024]{1,0:T(8,128)(2,1)} fusion(bf16[1024,1024]{1,0:T(8,128)(2,1)S(1)} %constant_dynamic-update-slice_fusion, bf16[256,1024]{1,0:T(8,128)(2,1)S(1)} %copy-done.1, s32[256,1024]{1,0:T(8,128)S(1)} %fusion.29, s32[256,1024]{1,0:T(8,128)S(1)} %fusion.30, s32[1024]{0:T(1024)S(1)} %bitcast.12, s32[256]{0:T(256)S(1)} %get-tuple-element.6), kind=kOutput, calls=%fused_computation.9 | convolution fusion | flops 543162368 | bytes 5248000 | tf_op jit(solution)/shard_map/dot_general | solution.py:60
  64.0 5.3 %convolution_convert_fusion = bf16[1024,1024]{1,0:T(8,128)(2,1)} fusion(bf16[256,1024]{1,0:T(8,128)(2,1)} %convolution_convert_fusion.1, bf16[1024,1024]{1,0:T(8,128)(2,1)} %all-gather.2.cloned.1.call-done, bf16[256,1024]{1,0:T(8,128)(2,1)} %gather_fusion, s32[256,1024]{1,0:T(8,128)} %copy-done, s32[256,1024]{1,0:T(8,128)S(1)} %fusion.29, ...), kind=kOutput, calls=%fused_computation.2 | convolution fusion | flops 1081081856 | bytes 7345152 | tf_op jit(solution)/shard_map/dot_general | solution.py:77
  (10 shorter events, 0.1 us)
Async XLA Ops:
  6.5 57.5 %all-gather.2.cloned.1.call-start = ((), (), s32[]{:S(2)}) async-start(), calls=%async_computation | async-start | bytes 2621440 | tf_op jit(solution)/shard_map/all_gather | solution.py:53
  7.3 18.5 %collective-permute-start = (bf16[256,1024]{1,0:T(8,128)(2,1)}, bf16[256,1024]{1,0:T(8,128)(2,1)}, u32[]{:S(2)}, u32[]{:S(2)}) collective-permute-start(bf16[256,1024]{1,0:T(8,128)(2,1)} %param.11), channel_id=1, source_target_pairs={{0,4},{4,8},{8,12},{12,0},{1,5},{5,9},{9,13},{13,1},{2,6},{6,10},{... | collective-permute-start | bytes 1572872 | tf_op jit(solution)/shard_map/ppermute | solution.py:13
  10.4 49.4 %collective-permute-start.1 = (bf16[256,1024]{1,0:T(8,128)(2,1)}, bf16[256,1024]{1,0:T(8,128)(2,1)}, u32[]{:S(2)}, u32[]{:S(2)}) collective-permute-start(bf16[256,1024]{1,0:T(8,128)(2,1)} %param.11), channel_id=1, source_target_pairs={{0,12},{4,0},{8,4},{12,8},{1,13},{5,1},{9,5},{13,9},{2,14},{6,2},{... | collective-permute-start | bytes 1572872 | tf_op jit(solution)/shard_map/ppermute | solution.py:16
  21.7 2.0 %copy-start.3 = (s32[256,10]{0,1:T(8,128)S(1)}, s32[256,10]{0,1:T(8,128)}, u32[]{:S(2)}) copy-start(s32[256,10]{0,1:T(8,128)} %param.14) | copy-start | bytes 30724
  21.7 2.0 %copy-start.5 = (s32[10]{0:T(128)S(1)}, s32[10]{0:T(128)}, u32[]{:S(2)}) copy-start(s32[10]{0:T(128)} %param.15) | copy-start | bytes 124
  23.7 2.0 %copy-start.2 = (bf16[256,1024]{1,0:T(8,128)(2,1)S(1)}, bf16[256,1024]{1,0:T(8,128)(2,1)}, u32[]{:S(2)}) copy-start(bf16[256,1024]{1,0:T(8,128)(2,1)} %param.11) | copy-start | bytes 1572868
  23.8 2.1 %copy-start.4 = (bf16[8,1024]{1,0:T(8,128)(2,1)S(1)}, bf16[8,1024]{1,0:T(8,128)(2,1)}, u32[]{:S(2)}) copy-start(bf16[8,1024]{1,0:T(8,128)(2,1)} %param.8) | copy-start | bytes 49156
  25.8 35.1 %collective-permute-start.2 = (bf16[256,1024]{1,0:T(8,128)(2,1)}, bf16[256,1024]{1,0:T(8,128)(2,1)}, u32[]{:S(2)}, u32[]{:S(2)}) collective-permute-start(bf16[256,1024]{1,0:T(8,128)(2,1)} %collective-permute-done), channel_id=1, source_target_pairs={{0,4},{4,8},{8,12},{12,0},{1,5},{5,9},{9,13},{13,1},{2,6},{6,10},{... | collective-permute-start | bytes 1572872 | tf_op jit(solution)/shard_map/ppermute | solution.py:13
  56.6 5.4 %copy-start.1 = (bf16[256,1024]{1,0:T(8,128)(2,1)S(1)}, bf16[256,1024]{1,0:T(8,128)(2,1)}, u32[]{:S(2)}) copy-start(bf16[256,1024]{1,0:T(8,128)(2,1)} %gather_fusion.1) | copy-start | bytes 1572868
  58.3 3.7 %copy-start = (s32[256,1024]{1,0:T(8,128)}, s32[256,1024]{1,0:T(8,128)S(1)}, u32[]{:S(2)}) copy-start(s32[256,1024]{1,0:T(8,128)S(1)} %fusion.30) | copy-start | bytes 3145732
Sparse Core Ops, SparseCore 0:
  8.9 25.2 all-gather.1
